TPU v7x, 32 devices: a whole 2x2x4 slice. The times are simulated.
32 devices in a mesh: grp: 2 (over x), had: 16 (over z, y, core).
Axes of the slice: x: 2, y: 2, z: 4, core: 2. Of those that a mesh axis runs over, the one named last changes fastest.
Arguments:
- source_slabs: bfloat16 [512, 128, 128], P(('grp', 'had')), parts along dimension 0, may hold values from -6 to 6
- sink_slabs: bfloat16 [512, 128, 128], P(('grp', 'had')), parts along dimension 0, may hold values from -6 to 6
- perambulators: bfloat16 [4, 2, 128, 128], P('grp'), parts along dimension 0, may hold values from -0.5 to 0.5
- send_pick: int32 [32, 16], P(('grp', 'had')), parts along dimension 0, may hold values from 0 to 15
- graph_slot: int32 [32, 512, 2], P(('grp', 'had')), parts along dimension 0, may hold values from 0 to 15
- graph_sink: int32 [32, 512, 2], P(('grp', 'had')), parts along dimension 0, may hold values from 0 to 15
- graph_count: int32 [32], P(('grp', 'had')), parts along dimension 0, may hold values from 64 to 512, as said below
- pair_list: int32 [256, 2], P(('grp', 'had')), parts along dimension 0, may hold values from 0 to 15
Outputs:
- edge_matrices: bfloat16 [32, 128, 128], P(('grp', 'had')), parts along dimension 0
- pair_products: bfloat16 [256, 128, 128], P(('grp', 'had')), parts along dimension 0
There are 2 independent parts, one for each index of `grp`. A program takes and returns all parts, laid end to end along the dimension named above; each array names one. Nothing has to cross between parts.
Inputs may be any that keep to these rules, and one draw needn't show every extreme that they name: Some reader uses all 512 graph slots; slots from graph_count on are unused.
All inputs are finite; a program needn't handle non-finite values.
Results may differ from a plain program's by a relative error of at most 0.012.
Values may be sent and summed in bfloat16 or wider, within the bound.
A program may use at most 64 MiB of HBM per device.

v0:
```python
import math
import jax
import jax.numpy as jnp
from jax import lax
from jax.sharding import PartitionSpec as P


def shards(
    source_slabs,
    sink_slabs,
    perambulators,
    send_pick,
    graph_slot,
    graph_sink,
    graph_count,
    pair_list,
):
    my_index = lax.axis_index("had")
    evecs = source_slabs.shape[1]
    per_device = source_slabs.shape[0]
    root_scale = 1.0 / math.sqrt(evecs)
    edge_scale = 1.0 / math.sqrt(evecs * graph_slot.shape[1])
    timeslice = my_index * per_device // evecs
    local_peram = lax.dynamic_index_in_dim(perambulators, timeslice, 0, keepdims=False)
    first_turn = jnp.einsum(
        "xa,jab->xjb", local_peram[0], source_slabs, preferred_element_type=jnp.float32
    ).astype(jnp.bfloat16)
    pick_row = send_pick[0]
    second_turn = jnp.einsum(
        "xjb,yb->xjy", first_turn, local_peram[1], preferred_element_type=jnp.float32
    ).astype(jnp.bfloat16)
    outgoing = jnp.take(second_turn, pick_row, axis=1)
    received = lax.all_to_all(outgoing, "had", split_axis=1, concat_axis=1, tiled=True)
    graph_rows = graph_slot.shape[1]
    block_width = min(64, graph_rows)
    slot_table = graph_slot[0]
    sink_table = graph_sink[0]
    graph_total = graph_count[0]

    def factor(slots, sinks):
        gathered = jnp.take(received, slots, axis=1)
        resident = jnp.take(sink_slabs, sinks, axis=0)
        product = jnp.einsum("gxb,agb->gxa", resident, gathered, preferred_element_type=jnp.float32)
        return (product * root_scale).astype(jnp.bfloat16)

    def accumulate(block_index, running_sum):
        offset = block_index * block_width
        slots = lax.dynamic_slice_in_dim(slot_table, offset, block_width, 0)
        sinks = lax.dynamic_slice_in_dim(sink_table, offset, block_width, 0)
        is_valid = (offset + jnp.arange(block_width, dtype=jnp.int32) < graph_total).astype(
            jnp.bfloat16
        )
        left_side = factor(slots[:, 0], sinks[:, 0]) * is_valid[:, None, None]
        right_side = factor(slots[:, 1], sinks[:, 1])
        return running_sum + jnp.einsum(
            "gxa,gay->xy", left_side, right_side, preferred_element_type=jnp.float32
        )

    block_count = (graph_total + block_width - 1) // block_width
    summed = lax.fori_loop(0, block_count, accumulate, jnp.zeros((evecs, evecs), jnp.float32))
    edge_local = (summed * edge_scale).astype(jnp.bfloat16)[None]
    left_ids = pair_list[:, 0]
    right_ids = pair_list[:, 1]
    shard_rows = lax.all_gather(edge_local, "had", axis=0, tiled=True)
    row_ids = jnp.arange(shard_rows.shape[0], dtype=jnp.int32)
    left_select = (left_ids[:, None] == row_ids[None, :]).astype(jnp.bfloat16)
    right_select = (right_ids[:, None] == row_ids[None, :]).astype(jnp.bfloat16)
    left_part = jnp.einsum(
        "pn,nxy->pxy", left_select, shard_rows, preferred_element_type=jnp.float32
    )
    right_part = jnp.einsum(
        "pn,nxy->pxy", right_select, shard_rows, preferred_element_type=jnp.float32
    )
    left_edges = left_part.astype(jnp.bfloat16)
    right_edges = right_part.astype(jnp.bfloat16)
    product = jnp.einsum(
        "pxa,pay->pxy", left_edges, right_edges, preferred_element_type=jnp.float32
    )
    pair_products = (product * root_scale).astype(jnp.bfloat16)
    return (edge_local, pair_products)


def solution(mesh):
    return jax.shard_map(
        shards,
        mesh=mesh,
        in_specs=(
            P(("grp", "had"), None, None),
            P(("grp", "had"), None, None),
            P("grp", None, None, None),
            P(("grp", "had"), None),
            P(("grp", "had"), None, None),
            P(("grp", "had"), None, None),
            P(("grp", "had")),
            P(("grp", "had"), None),
        ),
        out_specs=(P(("grp", "had"), None, None), P(("grp", "had"), None, None)),
        check_vma=False,
    )
```

profile of v0, /device:TPU:0, one launch (start us, length us, event | category | flops | bytes accessed | tf_op | source)
XLA Modules:
  0.0 210.6 jit_solution(10187311681063074676)
XLA Ops:
  0.6 0.0 copy-start
  0.7 0.7 fusion.45
  1.4 0.7 compare_and_fusion.4
  2.1 0.0 copy-start.2
  2.1 0.0 copy-start.1
  2.1 1.3 convolution_convert_fusion
  3.4 0.6 gather_fusion.4
  4.1 0.9 select_bitcast_fusion
  5.0 7.4 %all-to-all-start = ((bf16[128,16,128]{2,0,1:T(8,128)(2,1)}), bf16[128,16,128]{2,0,1:T(8,128)(2,1)S(1)}, u32[]{:S(2)}, u32[]{:S(2)}) async-start(bf16[128,16,128]{2,0,1:T(8,128)(2,1)} %select_bitcast_fusion), calls=%async_computation | async-start | bytes 1048576 | tf_op jit(solution)/shard_map/all_to_all | solution.py:33
  13.1 13.6 %all-to-all-done = bf16[128,16,128]{2,0,1:T(8,128)(2,1)S(1)} async-done(((bf16[128,16,128]{2,0,1:T(8,128)(2,1)}), bf16[128,16,128]{2,0,1:T(8,128)(2,1)S(1)}, u32[]{:S(2)}, u32[]{:S(2)}) %all-to-all-start) | async-done | bytes 524320 | tf_op jit(solution)/shard_map/all_to_all | solution.py:33
  26.7 81.4 %while.10 = (s32[]{:T(128)}, f32[128,128]{1,0:T(8,128)S(1)}, s32[]{:T(128)}, s32[512,2]{0,1:T(2,128)}, bf16[16,128,128]{2,1,0:T(8,128)(2,1)S(1)}, /*index=5*/s32...) while((s32[]{:T(128)}, f32[128,128]{1,0:T(8,128)S(1)}, ...), condition=%wide.region_1.4_spmd, body=%wide.region_0.3_spmd.sunk | while | flops 814765760 | bytes 29514672 | solution.py:60
  26.7 0.8 constant_dynamic-slice_fusion.3
  27.5 2.1 %gather_fusion = bf16[64,128,128]{2,1,0:T(8,128)(2,1)} fusion(bf16[128,16,128]{2,0,1:T(8,128)(2,1)S(1)} %get-tuple-element.188, s32[1024]{0:T(1024)S(1)} %pad_clamp_fusion.9), kind=kCustom, calls=%fused_computation.3.clone.clone.1 | custom fusion | bytes 4194560 | tf_op jit(solution)/shard_map/while/body/jit(_take)/gather | solution.py:41
  29.7 2.1 %gather_fusion.1 = bf16[64,128,128]{2,1,0:T(8,128)(2,1)} fusion(bf16[16,128,128]{2,1,0:T(8,128)(2,1)S(1)} %get-tuple-element.186, s32[1024]{0:T(1024)S(1)} %pad_clamp_fusion.10), kind=kCustom, calls=%fused_computation.2.clone.clone.1 | custom fusion | bytes 4194560 | tf_op jit(solution)/shard_map/while/body/jit(_take)/gather | solution.py:42
  31.8 5.2 %multiply_convert_fusion.4 = bf16[64,128,128]{2,1,0:T(8,128)(2,1)} fusion(bf16[64,128,128]{2,1,0:T(8,128)(2,1)} %gather_fusion, bf16[64,128,128]{2,1,0:T(8,128)(2,1)} %gather_fusion.1, pred[64]{0:T(512)(128)(4,1)S(1)} %get-tuple-element.152, pred[64]{0:T(512)(128)(4,1)S(1)} %get-tuple-element.153), kind=kOutput, calls=%fused_computation.5.clone.1 | convolution fusion | flops 272629760 | bytes 6291584 | tf_op jit(solution)/shard_map/while/body/gxb,agb->gxa/dot_general | solution.py:43
  37.0 2.1 %gather_fusion.2 = bf16[64,128,128]{2,1,0:T(8,128)(2,1)} fusion(bf16[128,16,128]{2,0,1:T(8,128)(2,1)S(1)} %get-tuple-element.188, s32[1024]{0:T(1024)S(1)} %pad_clamp_fusion.11), kind=kCustom, calls=%fused_computation.1.clone.clone.1 | custom fusion | bytes 4194560 | tf_op jit(solution)/shard_map/while/body/jit(_take)/gather | solution.py:41
  39.1 2.1 %gather_fusion.3 = bf16[64,128,128]{2,1,0:T(8,128)(2,1)} fusion(bf16[16,128,128]{2,1,0:T(8,128)(2,1)S(1)} %get-tuple-element.186, s32[1024]{0:T(1024)S(1)} %pad_clamp_fusion.12), kind=kCustom, calls=%fused_computation.clone.clone.1 | custom fusion | bytes 4194560 | tf_op jit(solution)/shard_map/while/body/jit(_take)/gather | solution.py:42
  41.3 0.6 compare_convert_fusion.2
  41.9 5.1 %fusion.64 = f32[128,128]{1,0:T(8,128)S(1)} fusion(f32[128,128]{1,0:T(8,128)S(1)} %get-tuple-element.171, bf16[64,128,128]{2,1,0:T(8,128)(2,1)} %multiply_convert_fusion.4, bf16[64,128,128]{2,1,0:T(8,128)(2,1)} %gather_fusion.2, bf16[64,128,128]{2,1,0:T(8,128)(2,1)} %gather_fusion.3, pred[64]{0:T(512)(128)(4,1)S(1)} %get-tuple-element.156, ...), kind=kOutput, calls=%fused_computation.20.clone.1 | convolution fusion | flops 542130176 | bytes 6422784 | tf_op jit(solution)/shard_map/while/body/gxa,gay->xy/dot_general | solution.py:55
  47.1 0.8 constant_dynamic-slice_fusion.3
  47.9 2.1 %gather_fusion = bf16[64,128,128]{2,1,0:T(8,128)(2,1)} fusion(bf16[128,16,128]{2,0,1:T(8,128)(2,1)S(1)} %get-tuple-element.188, s32[1024]{0:T(1024)S(1)} %pad_clamp_fusion.9), kind=kCustom, calls=%fused_computation.3.clone.clone.1 | custom fusion | bytes 4194560 | tf_op jit(solution)/shard_map/while/body/jit(_take)/gather | solution.py:41
  50.0 2.1 %gather_fusion.1 = bf16[64,128,128]{2,1,0:T(8,128)(2,1)} fusion(bf16[16,128,128]{2,1,0:T(8,128)(2,1)S(1)} %get-tuple-element.186, s32[1024]{0:T(1024)S(1)} %pad_clamp_fusion.10), kind=kCustom, calls=%fused_computation.2.clone.clone.1 | custom fusion | bytes 4194560 | tf_op jit(solution)/shard_map/while/body/jit(_take)/gather | solution.py:42
  52.1 5.2 %multiply_convert_fusion.4 = bf16[64,128,128]{2,1,0:T(8,128)(2,1)} fusion(bf16[64,128,128]{2,1,0:T(8,128)(2,1)} %gather_fusion, bf16[64,128,128]{2,1,0:T(8,128)(2,1)} %gather_fusion.1, pred[64]{0:T(512)(128)(4,1)S(1)} %get-tuple-element.152, pred[64]{0:T(512)(128)(4,1)S(1)} %get-tuple-element.153), kind=kOutput, calls=%fused_computation.5.clone.1 | convolution fusion | flops 272629760 | bytes 6291584 | tf_op jit(solution)/shard_map/while/body/gxb,agb->gxa/dot_general | solution.py:43
  57.4 2.1 %gather_fusion.2 = bf16[64,128,128]{2,1,0:T(8,128)(2,1)} fusion(bf16[128,16,128]{2,0,1:T(8,128)(2,1)S(1)} %get-tuple-element.188, s32[1024]{0:T(1024)S(1)} %pad_clamp_fusion.11), kind=kCustom, calls=%fused_computation.1.clone.clone.1 | custom fusion | bytes 4194560 | tf_op jit(solution)/shard_map/while/body/jit(_take)/gather | solution.py:41
  59.5 2.1 %gather_fusion.3 = bf16[64,128,128]{2,1,0:T(8,128)(2,1)} fusion(bf16[16,128,128]{2,1,0:T(8,128)(2,1)S(1)} %get-tuple-element.186, s32[1024]{0:T(1024)S(1)} %pad_clamp_fusion.12), kind=kCustom, calls=%fused_computation.clone.clone.1 | custom fusion | bytes 4194560 | tf_op jit(solution)/shard_map/while/body/jit(_take)/gather | solution.py:42
  61.6 0.6 compare_convert_fusion.2
  62.3 5.1 %fusion.64 = f32[128,128]{1,0:T(8,128)S(1)} fusion(f32[128,128]{1,0:T(8,128)S(1)} %get-tuple-element.171, bf16[64,128,128]{2,1,0:T(8,128)(2,1)} %multiply_convert_fusion.4, bf16[64,128,128]{2,1,0:T(8,128)(2,1)} %gather_fusion.2, bf16[64,128,128]{2,1,0:T(8,128)(2,1)} %gather_fusion.3, pred[64]{0:T(512)(128)(4,1)S(1)} %get-tuple-element.156, ...), kind=kOutput, calls=%fused_computation.20.clone.1 | convolution fusion | flops 542130176 | bytes 6422784 | tf_op jit(solution)/shard_map/while/body/gxa,gay->xy/dot_general | solution.py:55
  67.4 0.8 constant_dynamic-slice_fusion.3
  68.2 2.1 %gather_fusion = bf16[64,128,128]{2,1,0:T(8,128)(2,1)} fusion(bf16[128,16,128]{2,0,1:T(8,128)(2,1)S(1)} %get-tuple-element.188, s32[1024]{0:T(1024)S(1)} %pad_clamp_fusion.9), kind=kCustom, calls=%fused_computation.3.clone.clone.1 | custom fusion | bytes 4194560 | tf_op jit(solution)/shard_map/while/body/jit(_take)/gather | solution.py:41
  70.4 2.1 %gather_fusion.1 = bf16[64,128,128]{2,1,0:T(8,128)(2,1)} fusion(bf16[16,128,128]{2,1,0:T(8,128)(2,1)S(1)} %get-tuple-element.186, s32[1024]{0:T(1024)S(1)} %pad_clamp_fusion.10), kind=kCustom, calls=%fused_computation.2.clone.clone.1 | custom fusion | bytes 4194560 | tf_op jit(solution)/shard_map/while/body/jit(_take)/gather | solution.py:42
  72.5 5.2 %multiply_convert_fusion.4 = bf16[64,128,128]{2,1,0:T(8,128)(2,1)} fusion(bf16[64,128,128]{2,1,0:T(8,128)(2,1)} %gather_fusion, bf16[64,128,128]{2,1,0:T(8,128)(2,1)} %gather_fusion.1, pred[64]{0:T(512)(128)(4,1)S(1)} %get-tuple-element.152, pred[64]{0:T(512)(128)(4,1)S(1)} %get-tuple-element.153), kind=kOutput, calls=%fused_computation.5.clone.1 | convolution fusion | flops 272629760 | bytes 6291584 | tf_op jit(solution)/shard_map/while/body/gxb,agb->gxa/dot_general | solution.py:43
  77.7 2.1 %gather_fusion.2 = bf16[64,128,128]{2,1,0:T(8,128)(2,1)} fusion(bf16[128,16,128]{2,0,1:T(8,128)(2,1)S(1)} %get-tuple-element.188, s32[1024]{0:T(1024)S(1)} %pad_clamp_fusion.11), kind=kCustom, calls=%fused_computation.1.clone.clone.1 | custom fusion | bytes 4194560 | tf_op jit(solution)/shard_map/while/body/jit(_take)/gather | solution.py:41
  79.8 2.1 %gather_fusion.3 = bf16[64,128,128]{2,1,0:T(8,128)(2,1)} fusion(bf16[16,128,128]{2,1,0:T(8,128)(2,1)S(1)} %get-tuple-element.186, s32[1024]{0:T(1024)S(1)} %pad_clamp_fusion.12), kind=kCustom, calls=%fused_computation.clone.clone.1 | custom fusion | bytes 4194560 | tf_op jit(solution)/shard_map/while/body/jit(_take)/gather | solution.py:42
  82.0 0.6 compare_convert_fusion.2
  82.6 5.1 %fusion.64 = f32[128,128]{1,0:T(8,128)S(1)} fusion(f32[128,128]{1,0:T(8,128)S(1)} %get-tuple-element.171, bf16[64,128,128]{2,1,0:T(8,128)(2,1)} %multiply_convert_fusion.4, bf16[64,128,128]{2,1,0:T(8,128)(2,1)} %gather_fusion.2, bf16[64,128,128]{2,1,0:T(8,128)(2,1)} %gather_fusion.3, pred[64]{0:T(512)(128)(4,1)S(1)} %get-tuple-element.156, ...), kind=kOutput, calls=%fused_computation.20.clone.1 | convolution fusion | flops 542130176 | bytes 6422784 | tf_op jit(solution)/shard_map/while/body/gxa,gay->xy/dot_general | solution.py:55
  87.8 0.8 constant_dynamic-slice_fusion.3
  88.6 2.1 %gather_fusion = bf16[64,128,128]{2,1,0:T(8,128)(2,1)} fusion(bf16[128,16,128]{2,0,1:T(8,128)(2,1)S(1)} %get-tuple-element.188, s32[1024]{0:T(1024)S(1)} %pad_clamp_fusion.9), kind=kCustom, calls=%fused_computation.3.clone.clone.1 | custom fusion | bytes 4194560 | tf_op jit(solution)/shard_map/while/body/jit(_take)/gather | solution.py:41
  90.7 2.1 %gather_fusion.1 = bf16[64,128,128]{2,1,0:T(8,128)(2,1)} fusion(bf16[16,128,128]{2,1,0:T(8,128)(2,1)S(1)} %get-tuple-element.186, s32[1024]{0:T(1024)S(1)} %pad_clamp_fusion.10), kind=kCustom, calls=%fused_computation.2.clone.clone.1 | custom fusion | bytes 4194560 | tf_op jit(solution)/shard_map/while/body/jit(_take)/gather | solution.py:42
  92.8 5.2 %multiply_convert_fusion.4 = bf16[64,128,128]{2,1,0:T(8,128)(2,1)} fusion(bf16[64,128,128]{2,1,0:T(8,128)(2,1)} %gather_fusion, bf16[64,128,128]{2,1,0:T(8,128)(2,1)} %gather_fusion.1, pred[64]{0:T(512)(128)(4,1)S(1)} %get-tuple-element.152, pred[64]{0:T(512)(128)(4,1)S(1)} %get-tuple-element.153), kind=kOutput, calls=%fused_computation.5.clone.1 | convolution fusion | flops 272629760 | bytes 6291584 | tf_op jit(solution)/shard_map/while/body/gxb,agb->gxa/dot_general | solution.py:43
  98.1 2.1 %gather_fusion.2 = bf16[64,128,128]{2,1,0:T(8,128)(2,1)} fusion(bf16[128,16,128]{2,0,1:T(8,128)(2,1)S(1)} %get-tuple-element.188, s32[1024]{0:T(1024)S(1)} %pad_clamp_fusion.11), kind=kCustom, calls=%fused_computation.1.clone.clone.1 | custom fusion | bytes 4194560 | tf_op jit(solution)/shard_map/while/body/jit(_take)/gather | solution.py:41
  100.2 2.1 %gather_fusion.3 = bf16[64,128,128]{2,1,0:T(8,128)(2,1)} fusion(bf16[16,128,128]{2,1,0:T(8,128)(2,1)S(1)} %get-tuple-element.186, s32[1024]{0:T(1024)S(1)} %pad_clamp_fusion.12), kind=kCustom, calls=%fused_computation.clone.clone.1 | custom fusion | bytes 4194560 | tf_op jit(solution)/shard_map/while/body/jit(_take)/gather | solution.py:42
  102.3 0.6 compare_convert_fusion.2
  103.0 5.1 %fusion.64 = f32[128,128]{1,0:T(8,128)S(1)} fusion(f32[128,128]{1,0:T(8,128)S(1)} %get-tuple-element.171, bf16[64,128,128]{2,1,0:T(8,128)(2,1)} %multiply_convert_fusion.4, bf16[64,128,128]{2,1,0:T(8,128)(2,1)} %gather_fusion.2, bf16[64,128,128]{2,1,0:T(8,128)(2,1)} %gather_fusion.3, pred[64]{0:T(512)(128)(4,1)S(1)} %get-tuple-element.156, ...), kind=kOutput, calls=%fused_computation.20.clone.1 | convolution fusion | flops 542130176 | bytes 6422784 | tf_op jit(solution)/shard_map/while/body/gxa,gay->xy/dot_general | solution.py:55
  108.1 0.6 fusion.50
  108.7 100.1 %all-gather = bf16[2048,128]{1,0:T(8,128)(2,1)S(1)} all-gather(bf16[128,128]{1,0:T(8,128)(2,1)S(1)} %multiply_convert_fusion.2), channel_id=2, replica_groups=mesh['grp'=2,'had'=16] {'had'}, dimensions={0}, use_global_device_ids=true | all-gather | bytes 557056 | tf_op jit(solution)/shard_map/all_gather | solution.py:64
  208.8 0.4 fusion.35
  209.2 0.4 fusion.37
  209.6 0.9 fusion.34
  (31 shorter events, 0.2 us)
Async XLA Ops:
  0.6 1.4 copy-start
  2.1 11.0 %copy-start.2 = (s32[8,2]{0,1:T(2,128)S(1)}, s32[8,2]{0,1:T(2,128)}, u32[]{:S(2)}) copy-start(s32[8,2]{0,1:T(2,128)} %param.21) | copy-start | bytes 196
  2.1 24.6 %copy-start.1 = (bf16[16,128,128]{2,1,0:T(8,128)(2,1)S(1)}, bf16[16,128,128]{2,1,0:T(8,128)(2,1)}, u32[]{:S(2)}) copy-start(bf16[16,128,128]{2,1,0:T(8,128)(2,1)} %param.15) | copy-start | bytes 1572868
  5.0 21.7 %all-to-all-start = ((bf16[128,16,128]{2,0,1:T(8,128)(2,1)}), bf16[128,16,128]{2,0,1:T(8,128)(2,1)S(1)}, u32[]{:S(2)}, u32[]{:S(2)}) async-start(bf16[128,16,128]{2,0,1:T(8,128)(2,1)} %select_bitcast_fusion), calls=%async_computation | async-start | bytes 1048576 | tf_op jit(solution)/shard_map/all_to_all | solution.py:33
where the time goes:
time: 211 us
  blocking collectives  100 us (47%)
  matrix products  44.2 us (21%)
  local copies, waits for them, and re-layouts  37.9 us (18%)
  waiting for transfers between devices  13.6 us (6%)
  starting transfers between devices  7.41 us (4%)
  other arithmetic  5.68 us (3%)
    all_gather x1, blocking collectives, shards(): shard_rows = lax.all_gather(edge_local, 'had', axis=0, tiled=True)  100 us
    dot_general x4, matrix products, factor(): jnp.einsum('gxb,agb->gxa', resident, gathered, preferred_element_type=jnp...  20.8 us
    dot_general x4, matrix products, accumulate(): jnp.einsum('gxa,gay->xy', left_side, right_side, preferred_element_type=j...  20.3 us
    gather x8, local copies, waits for them, and re-layouts, factor(): resident = jnp.take(sink_slabs, sinks, axis=0)  17.1 us
    gather x8, local copies, waits for them, and re-layouts, factor(): gathered = jnp.take(received, slots, axis=1)  17.1 us
    all_to_all x1, waiting for transfers between devices, shards(): lax.all_to_all(outgoing, 'had', split_axis=1, concat_axis=1, tiled=True)  13.6 us
    all_to_all x1, starting transfers between devices, shards(): lax.all_to_all(outgoing, 'had', split_axis=1, concat_axis=1, tiled=True)  7.41 us
  transfers between devices with their start and end apart: 1, of which 1 were waited for; matrix products, arithmetic and copies ran while one was open for 0% of the time, Pallas kernels for 0%

commit v1 on v0

--- a/solution.py
+++ b/solution.py
@@ -3,6 +3,11 @@
 import jax.numpy as jnp
 from jax import lax
 from jax.sharding import PartitionSpec as P
+
+
+def exchange_gather(shard, mesh_axis, along):
+    sent = jnp.stack([shard] * lax.axis_size(mesh_axis))
+    return jnp.concatenate(lax.all_to_all(sent, mesh_axis, 0, 0), axis=along)
 
 
 def shards(
@@ -61,7 +66,7 @@
     edge_local = (summed * edge_scale).astype(jnp.bfloat16)[None]
     left_ids = pair_list[:, 0]
     right_ids = pair_list[:, 1]
-    shard_rows = lax.all_gather(edge_local, "had", axis=0, tiled=True)
+    shard_rows = exchange_gather(edge_local, "had", 0)
     row_ids = jnp.arange(shard_rows.shape[0], dtype=jnp.int32)
     left_select = (left_ids[:, None] == row_ids[None, :]).astype(jnp.bfloat16)
     right_select = (right_ids[:, None] == row_ids[None, :]).astype(jnp.bfloat16)

time: 211 us -> 210 us (level)
  blocking collectives: 100 us -> 0 us
  starting transfers between devices: 7.41 us -> 92.1 us
  waiting for transfers between devices: 13.6 us -> 27.2 us
    all_gather x1 -> x0, blocking collectives: 100 us -> none  [shards(): shard_rows = lax.all_gather(edge_local, 'had', axis=0, tiled=True)]
    all_to_all x0 -> x1, starting transfers between devices: none -> 84.7 us  [exchange_gather(): return jnp.concatenate(lax.all_to_all(sent, mesh_axis, 0, 0), axis=along)]
    all_to_all x0 -> x1, waiting for transfers between devices: none -> 13.6 us  [exchange_gather(): return jnp.concatenate(lax.all_to_all(sent, mesh_axis, 0, 0), axis=along)]
  transfers between devices with their start and end apart: 1 -> 2, of which waited for: 1 -> 2; matrix products, arithmetic and copies ran while one was open for 0% -> 0% of each run, Pallas kernels for 0% -> 0%
where the time goes in v1:
time: 210 us
  starting transfers between devices  92.1 us (44%)
  matrix products  44.2 us (21%)
  local copies, waits for them, and re-layouts  38.8 us (18%)
  waiting for transfers between devices  27.2 us (13%)
  other arithmetic  5.67 us (3%)
    all_to_all x1, starting transfers between devices, exchange_gather(): return jnp.concatenate(lax.all_to_all(sent, mesh_axis, 0, 0), axis=along)  84.7 us
    dot_general x4, matrix products, factor(): jnp.einsum('gxb,agb->gxa', resident, gathered, preferred_element_type=jnp...  20.8 us
    dot_general x4, matrix products, accumulate(): jnp.einsum('gxa,gay->xy', left_side, right_side, preferred_element_type=j...  20.4 us
    gather x8, local copies, waits for them, and re-layouts, factor(): resident = jnp.take(sink_slabs, sinks, axis=0)  17.1 us
    gather x8, local copies, waits for them, and re-layouts, factor(): gathered = jnp.take(received, slots, axis=1)  17.1 us
    all_to_all x1, waiting for transfers between devices, exchange_gather(): return jnp.concatenate(lax.all_to_all(sent, mesh_axis, 0, 0), axis=along)  13.6 us
    all_to_all x1, waiting for transfers between devices, shards(): lax.all_to_all(outgoing, 'had', split_axis=1, concat_axis=1, tiled=True)  13.6 us
    all_to_all x1, starting transfers between devices, shards(): lax.all_to_all(outgoing, 'had', split_axis=1, concat_axis=1, tiled=True)  7.41 us
  transfers between devices with their start and end apart: 2, of which 2 were waited for; matrix products, arithmetic and copies ran while one was open for 0% of the time, Pallas kernels for 0%

profile of v1, /device:TPU:0, one launch (start us, length us, event | category | flops | bytes accessed | tf_op | source)
XLA Modules:
  0.0 209.7 jit_solution(10302668252594414979)
XLA Ops:
  0.6 0.0 copy-start
  0.7 0.7 fusion.45
  1.4 0.7 compare_and_fusion.4
  2.1 1.3 convolution_convert_fusion
  3.4 0.6 gather_fusion.4
  4.0 0.9 select_bitcast_fusion
  5.0 7.4 %all-to-all-start = ((bf16[128,16,128]{2,0,1:T(8,128)(2,1)}), bf16[128,16,128]{2,0,1:T(8,128)(2,1)S(1)}, u32[]{:S(2)}, u32[]{:S(2)}) async-start(bf16[128,16,128]{2,0,1:T(8,128)(2,1)} %select_bitcast_fusion), calls=%async_computation | async-start | bytes 1048576 | tf_op jit(solution)/shard_map/all_to_all | solution.py:38
  13.0 13.6 %all-to-all-done = bf16[128,16,128]{2,0,1:T(8,128)(2,1)S(1)} async-done(((bf16[128,16,128]{2,0,1:T(8,128)(2,1)}), bf16[128,16,128]{2,0,1:T(8,128)(2,1)S(1)}, u32[]{:S(2)}, u32[]{:S(2)}) %all-to-all-start) | async-done | bytes 524320 | tf_op jit(solution)/shard_map/all_to_all | solution.py:38
  26.7 81.4 %while.10 = (s32[]{:T(128)}, f32[128,128]{1,0:T(8,128)S(1)}, s32[]{:T(128)}, s32[512,2]{0,1:T(2,128)}, bf16[16,128,128]{2,1,0:T(8,128)(2,1)S(1)}, /*index=5*/s32...) while((s32[]{:T(128)}, f32[128,128]{1,0:T(8,128)S(1)}, ...), condition=%wide.region_1.4_spmd, body=%wide.region_0.3_spmd.sunk | while | flops 814765760 | bytes 29514672 | solution.py:65
  26.7 0.8 constant_dynamic-slice_fusion.3
  27.5 2.1 %gather_fusion = bf16[64,128,128]{2,1,0:T(8,128)(2,1)} fusion(bf16[128,16,128]{2,0,1:T(8,128)(2,1)S(1)} %get-tuple-element.188, s32[1024]{0:T(1024)S(1)} %pad_clamp_fusion.9), kind=kCustom, calls=%fused_computation.3.clone.clone.1 | custom fusion | bytes 4194560 | tf_op jit(solution)/shard_map/while/body/jit(_take)/gather | solution.py:46
  29.7 2.1 %gather_fusion.1 = bf16[64,128,128]{2,1,0:T(8,128)(2,1)} fusion(bf16[16,128,128]{2,1,0:T(8,128)(2,1)S(1)} %get-tuple-element.186, s32[1024]{0:T(1024)S(1)} %pad_clamp_fusion.10), kind=kCustom, calls=%fused_computation.2.clone.clone.1 | custom fusion | bytes 4194560 | tf_op jit(solution)/shard_map/while/body/jit(_take)/gather | solution.py:47
  31.8 5.2 %multiply_convert_fusion.4 = bf16[64,128,128]{2,1,0:T(8,128)(2,1)} fusion(bf16[64,128,128]{2,1,0:T(8,128)(2,1)} %gather_fusion, bf16[64,128,128]{2,1,0:T(8,128)(2,1)} %gather_fusion.1, pred[64]{0:T(512)(128)(4,1)S(1)} %get-tuple-element.152, pred[64]{0:T(512)(128)(4,1)S(1)} %get-tuple-element.153), kind=kOutput, calls=%fused_computation.5.clone.1 | convolution fusion | flops 272629760 | bytes 6291584 | tf_op jit(solution)/shard_map/while/body/gxb,agb->gxa/dot_general | solution.py:48
  37.0 2.1 %gather_fusion.2 = bf16[64,128,128]{2,1,0:T(8,128)(2,1)} fusion(bf16[128,16,128]{2,0,1:T(8,128)(2,1)S(1)} %get-tuple-element.188, s32[1024]{0:T(1024)S(1)} %pad_clamp_fusion.11), kind=kCustom, calls=%fused_computation.1.clone.clone.1 | custom fusion | bytes 4194560 | tf_op jit(solution)/shard_map/while/body/jit(_take)/gather | solution.py:46
  39.1 2.1 %gather_fusion.3 = bf16[64,128,128]{2,1,0:T(8,128)(2,1)} fusion(bf16[16,128,128]{2,1,0:T(8,128)(2,1)S(1)} %get-tuple-element.186, s32[1024]{0:T(1024)S(1)} %pad_clamp_fusion.12), kind=kCustom, calls=%fused_computation.clone.clone.1 | custom fusion | bytes 4194560 | tf_op jit(solution)/shard_map/while/body/jit(_take)/gather | solution.py:47
  41.3 0.6 compare_convert_fusion.2
  41.9 5.1 %fusion.64 = f32[128,128]{1,0:T(8,128)S(1)} fusion(f32[128,128]{1,0:T(8,128)S(1)} %get-tuple-element.171, bf16[64,128,128]{2,1,0:T(8,128)(2,1)} %multiply_convert_fusion.4, bf16[64,128,128]{2,1,0:T(8,128)(2,1)} %gather_fusion.2, bf16[64,128,128]{2,1,0:T(8,128)(2,1)} %gather_fusion.3, pred[64]{0:T(512)(128)(4,1)S(1)} %get-tuple-element.156, ...), kind=kOutput, calls=%fused_computation.20.clone.1 | convolution fusion | flops 542130176 | bytes 6422784 | tf_op jit(solution)/shard_map/while/body/gxa,gay->xy/dot_general | solution.py:60
  47.0 0.8 constant_dynamic-slice_fusion.3
  47.8 2.1 %gather_fusion = bf16[64,128,128]{2,1,0:T(8,128)(2,1)} fusion(bf16[128,16,128]{2,0,1:T(8,128)(2,1)S(1)} %get-tuple-element.188, s32[1024]{0:T(1024)S(1)} %pad_clamp_fusion.9), kind=kCustom, calls=%fused_computation.3.clone.clone.1 | custom fusion | bytes 4194560 | tf_op jit(solution)/shard_map/while/body/jit(_take)/gather | solution.py:46
  50.0 2.1 %gather_fusion.1 = bf16[64,128,128]{2,1,0:T(8,128)(2,1)} fusion(bf16[16,128,128]{2,1,0:T(8,128)(2,1)S(1)} %get-tuple-element.186, s32[1024]{0:T(1024)S(1)} %pad_clamp_fusion.10), kind=kCustom, calls=%fused_computation.2.clone.clone.1 | custom fusion | bytes 4194560 | tf_op jit(solution)/shard_map/while/body/jit(_take)/gather | solution.py:47
  52.1 5.2 %multiply_convert_fusion.4 = bf16[64,128,128]{2,1,0:T(8,128)(2,1)} fusion(bf16[64,128,128]{2,1,0:T(8,128)(2,1)} %gather_fusion, bf16[64,128,128]{2,1,0:T(8,128)(2,1)} %gather_fusion.1, pred[64]{0:T(512)(128)(4,1)S(1)} %get-tuple-element.152, pred[64]{0:T(512)(128)(4,1)S(1)} %get-tuple-element.153), kind=kOutput, calls=%fused_computation.5.clone.1 | convolution fusion | flops 272629760 | bytes 6291584 | tf_op jit(solution)/shard_map/while/body/gxb,agb->gxa/dot_general | solution.py:48
  57.4 2.1 %gather_fusion.2 = bf16[64,128,128]{2,1,0:T(8,128)(2,1)} fusion(bf16[128,16,128]{2,0,1:T(8,128)(2,1)S(1)} %get-tuple-element.188, s32[1024]{0:T(1024)S(1)} %pad_clamp_fusion.11), kind=kCustom, calls=%fused_computation.1.clone.clone.1 | custom fusion | bytes 4194560 | tf_op jit(solution)/shard_map/while/body/jit(_take)/gather | solution.py:46
  59.5 2.1 %gather_fusion.3 = bf16[64,128,128]{2,1,0:T(8,128)(2,1)} fusion(bf16[16,128,128]{2,1,0:T(8,128)(2,1)S(1)} %get-tuple-element.186, s32[1024]{0:T(1024)S(1)} %pad_clamp_fusion.12), kind=kCustom, calls=%fused_computation.clone.clone.1 | custom fusion | bytes 4194560 | tf_op jit(solution)/shard_map/while/body/jit(_take)/gather | solution.py:47
  61.6 0.6 compare_convert_fusion.2
  62.3 5.1 %fusion.64 = f32[128,128]{1,0:T(8,128)S(1)} fusion(f32[128,128]{1,0:T(8,128)S(1)} %get-tuple-element.171, bf16[64,128,128]{2,1,0:T(8,128)(2,1)} %multiply_convert_fusion.4, bf16[64,128,128]{2,1,0:T(8,128)(2,1)} %gather_fusion.2, bf16[64,128,128]{2,1,0:T(8,128)(2,1)} %gather_fusion.3, pred[64]{0:T(512)(128)(4,1)S(1)} %get-tuple-element.156, ...), kind=kOutput, calls=%fused_computation.20.clone.1 | convolution fusion | flops 542130176 | bytes 6422784 | tf_op jit(solution)/shard_map/while/body/gxa,gay->xy/dot_general | solution.py:60
  67.4 0.8 constant_dynamic-slice_fusion.3
  68.2 2.1 %gather_fusion = bf16[64,128,128]{2,1,0:T(8,128)(2,1)} fusion(bf16[128,16,128]{2,0,1:T(8,128)(2,1)S(1)} %get-tuple-element.188, s32[1024]{0:T(1024)S(1)} %pad_clamp_fusion.9), kind=kCustom, calls=%fused_computation.3.clone.clone.1 | custom fusion | bytes 4194560 | tf_op jit(solution)/shard_map/while/body/jit(_take)/gather | solution.py:46
  70.4 2.1 %gather_fusion.1 = bf16[64,128,128]{2,1,0:T(8,128)(2,1)} fusion(bf16[16,128,128]{2,1,0:T(8,128)(2,1)S(1)} %get-tuple-element.186, s32[1024]{0:T(1024)S(1)} %pad_clamp_fusion.10), kind=kCustom, calls=%fused_computation.2.clone.clone.1 | custom fusion | bytes 4194560 | tf_op jit(solution)/shard_map/while/body/jit(_take)/gather | solution.py:47
  72.5 5.2 %multiply_convert_fusion.4 = bf16[64,128,128]{2,1,0:T(8,128)(2,1)} fusion(bf16[64,128,128]{2,1,0:T(8,128)(2,1)} %gather_fusion, bf16[64,128,128]{2,1,0:T(8,128)(2,1)} %gather_fusion.1, pred[64]{0:T(512)(128)(4,1)S(1)} %get-tuple-element.152, pred[64]{0:T(512)(128)(4,1)S(1)} %get-tuple-element.153), kind=kOutput, calls=%fused_computation.5.clone.1 | convolution fusion | flops 272629760 | bytes 6291584 | tf_op jit(solution)/shard_map/while/body/gxb,agb->gxa/dot_general | solution.py:48
  77.7 2.1 %gather_fusion.2 = bf16[64,128,128]{2,1,0:T(8,128)(2,1)} fusion(bf16[128,16,128]{2,0,1:T(8,128)(2,1)S(1)} %get-tuple-element.188, s32[1024]{0:T(1024)S(1)} %pad_clamp_fusion.11), kind=kCustom, calls=%fused_computation.1.clone.clone.1 | custom fusion | bytes 4194560 | tf_op jit(solution)/shard_map/while/body/jit(_take)/gather | solution.py:46
  79.9 2.1 %gather_fusion.3 = bf16[64,128,128]{2,1,0:T(8,128)(2,1)} fusion(bf16[16,128,128]{2,1,0:T(8,128)(2,1)S(1)} %get-tuple-element.186, s32[1024]{0:T(1024)S(1)} %pad_clamp_fusion.12), kind=kCustom, calls=%fused_computation.clone.clone.1 | custom fusion | bytes 4194560 | tf_op jit(solution)/shard_map/while/body/jit(_take)/gather | solution.py:47
  82.0 0.6 compare_convert_fusion.2
  82.6 5.1 %fusion.64 = f32[128,128]{1,0:T(8,128)S(1)} fusion(f32[128,128]{1,0:T(8,128)S(1)} %get-tuple-element.171, bf16[64,128,128]{2,1,0:T(8,128)(2,1)} %multiply_convert_fusion.4, bf16[64,128,128]{2,1,0:T(8,128)(2,1)} %gather_fusion.2, bf16[64,128,128]{2,1,0:T(8,128)(2,1)} %gather_fusion.3, pred[64]{0:T(512)(128)(4,1)S(1)} %get-tuple-element.156, ...), kind=kOutput, calls=%fused_computation.20.clone.1 | convolution fusion | flops 542130176 | bytes 6422784 | tf_op jit(solution)/shard_map/while/body/gxa,gay->xy/dot_general | solution.py:60
  87.8 0.8 constant_dynamic-slice_fusion.3
  88.6 2.1 %gather_fusion = bf16[64,128,128]{2,1,0:T(8,128)(2,1)} fusion(bf16[128,16,128]{2,0,1:T(8,128)(2,1)S(1)} %get-tuple-element.188, s32[1024]{0:T(1024)S(1)} %pad_clamp_fusion.9), kind=kCustom, calls=%fused_computation.3.clone.clone.1 | custom fusion | bytes 4194560 | tf_op jit(solution)/shard_map/while/body/jit(_take)/gather | solution.py:46
  90.7 2.1 %gather_fusion.1 = bf16[64,128,128]{2,1,0:T(8,128)(2,1)} fusion(bf16[16,128,128]{2,1,0:T(8,128)(2,1)S(1)} %get-tuple-element.186, s32[1024]{0:T(1024)S(1)} %pad_clamp_fusion.10), kind=kCustom, calls=%fused_computation.2.clone.clone.1 | custom fusion | bytes 4194560 | tf_op jit(solution)/shard_map/while/body/jit(_take)/gather | solution.py:47
  92.9 5.2 %multiply_convert_fusion.4 = bf16[64,128,128]{2,1,0:T(8,128)(2,1)} fusion(bf16[64,128,128]{2,1,0:T(8,128)(2,1)} %gather_fusion, bf16[64,128,128]{2,1,0:T(8,128)(2,1)} %gather_fusion.1, pred[64]{0:T(512)(128)(4,1)S(1)} %get-tuple-element.152, pred[64]{0:T(512)(128)(4,1)S(1)} %get-tuple-element.153), kind=kOutput, calls=%fused_computation.5.clone.1 | convolution fusion | flops 272629760 | bytes 6291584 | tf_op jit(solution)/shard_map/while/body/gxb,agb->gxa/dot_general | solution.py:48
  98.1 2.1 %gather_fusion.2 = bf16[64,128,128]{2,1,0:T(8,128)(2,1)} fusion(bf16[128,16,128]{2,0,1:T(8,128)(2,1)S(1)} %get-tuple-element.188, s32[1024]{0:T(1024)S(1)} %pad_clamp_fusion.11), kind=kCustom, calls=%fused_computation.1.clone.clone.1 | custom fusion | bytes 4194560 | tf_op jit(solution)/shard_map/while/body/jit(_take)/gather | solution.py:46
  100.2 2.1 %gather_fusion.3 = bf16[64,128,128]{2,1,0:T(8,128)(2,1)} fusion(bf16[16,128,128]{2,1,0:T(8,128)(2,1)S(1)} %get-tuple-element.186, s32[1024]{0:T(1024)S(1)} %pad_clamp_fusion.12), kind=kCustom, calls=%fused_computation.clone.clone.1 | custom fusion | bytes 4194560 | tf_op jit(solution)/shard_map/while/body/jit(_take)/gather | solution.py:47
  102.3 0.6 compare_convert_fusion.2
  103.0 5.1 %fusion.64 = f32[128,128]{1,0:T(8,128)S(1)} fusion(f32[128,128]{1,0:T(8,128)S(1)} %get-tuple-element.171, bf16[64,128,128]{2,1,0:T(8,128)(2,1)} %multiply_convert_fusion.4, bf16[64,128,128]{2,1,0:T(8,128)(2,1)} %gather_fusion.2, bf16[64,128,128]{2,1,0:T(8,128)(2,1)} %gather_fusion.3, pred[64]{0:T(512)(128)(4,1)S(1)} %get-tuple-element.156, ...), kind=kOutput, calls=%fused_computation.20.clone.1 | convolution fusion | flops 542130176 | bytes 6422784 | tf_op jit(solution)/shard_map/while/body/gxa,gay->xy/dot_general | solution.py:60
  108.1 0.9 stack.3
  109.0 84.7 %all-to-all-start.1 = ((bf16[16,1,128,128]{3,2,1,0:T(8,128)(2,1)}), bf16[16,1,128,128]{3,2,1,0:T(8,128)(2,1)S(1)}, u32[]{:S(2)}, u32[]{:S(2)}) async-start(bf16[16,1,128,128]{3,2,1,0:T(8,128)(2,1)} %stack.3), calls=%async_computation.1 | async-start | bytes 1048576 | tf_op jit(solution)/shard_map/all_to_all | solution.py:10
  193.7 0.6 fusion.50
  194.3 13.6 %all-to-all-done.1 = bf16[16,1,128,128]{3,2,1,0:T(8,128)(2,1)S(1)} async-done(((bf16[16,1,128,128]{3,2,1,0:T(8,128)(2,1)}), bf16[16,1,128,128]{3,2,1,0:T(8,128)(2,1)S(1)}, u32[]{:S(2)}, u32[]{:S(2)}) %all-to-all-start.1) | async-done | bytes 524320 | tf_op jit(solution)/shard_map/all_to_all | solution.py:10
  207.9 0.4 fusion.35
  208.3 0.4 fusion.37
  208.8 0.9 fusion.34
  (33 shorter events, 0.2 us)
Async XLA Ops:
  0.6 1.4 copy-start
  2.1 24.6 %copy-start.1 = (bf16[16,128,128]{2,1,0:T(8,128)(2,1)S(1)}, bf16[16,128,128]{2,1,0:T(8,128)(2,1)}, u32[]{:S(2)}) copy-start(bf16[16,128,128]{2,1,0:T(8,128)(2,1)} %param.15) | copy-start | bytes 1572868
  5.0 21.7 %all-to-all-start = ((bf16[128,16,128]{2,0,1:T(8,128)(2,1)}), bf16[128,16,128]{2,0,1:T(8,128)(2,1)S(1)}, u32[]{:S(2)}, u32[]{:S(2)}) async-start(bf16[128,16,128]{2,0,1:T(8,128)(2,1)} %select_bitcast_fusion), calls=%async_computation | async-start | bytes 1048576 | tf_op jit(solution)/shard_map/all_to_all | solution.py:38
  26.7 167.0 %copy-start.2 = (s32[8,2]{0,1:T(2,128)S(1)}, s32[8,2]{0,1:T(2,128)}, u32[]{:S(2)}) copy-start(s32[8,2]{0,1:T(2,128)} %param.21) | copy-start | bytes 196
  109.0 98.9 %all-to-all-start.1 = ((bf16[16,1,128,128]{3,2,1,0:T(8,128)(2,1)}), bf16[16,1,128,128]{3,2,1,0:T(8,128)(2,1)S(1)}, u32[]{:S(2)}, u32[]{:S(2)}) async-start(bf16[16,1,128,128]{3,2,1,0:T(8,128)(2,1)} %stack.3), calls=%async_computation.1 | async-start | bytes 1048576 | tf_op jit(solution)/shard_map/all_to_all | solution.py:10
